TPU v7x, 32 devices: a whole 2x2x4 slice. The times are simulated.
32 devices in a mesh: groups: 2 (over y), row: 4 (over z), col: 4 (over x, core).
Axes of the slice: x: 2, y: 2, z: 4, core: 2. Of those that a mesh axis runs over, the one named last changes fastest.
Arguments:
- seq_feat: bfloat16 [64, 256], P(('groups', 'row', 'col')), parts along dimension 0, may hold values from -6 to 6
- lengths: int32 [4], P('groups'), parts along dimension 0, may hold values from 1 to 24, 32 in all
- embed_weight: bfloat16 [2, 256, 128], replicated, may hold values from -0.375 to 0.375
- norm_gain: float32 [4, 128], replicated, may hold values from 0.1 to 1.9
- conv_weight: bfloat16 [4, 3, 3, 128, 128], replicated, may hold values from -0.1875 to 0.1875
- proj_weight: bfloat16 [4, 128, 128], replicated, may hold values from -0.5 to 0.5
- pair_cotangent: bfloat16 [64, 32, 128], P(('groups', 'row'), 'col'), parts along dimension 0, may hold values from -13 to 13
Outputs:
- pair_output: bfloat16 [64, 32, 128], P(('groups', 'row'), 'col'), parts along dimension 0
- seq_grad: float32 [64, 256], P(('groups', 'row', 'col')), parts along dimension 0
- embed_grad: float32 [4, 256, 128], P('groups'), parts along dimension 0
- gain_grad: float32 [8, 128], P('groups'), parts along dimension 0
- conv_grad: float32 [8, 3, 3, 128, 128], P('groups'), parts along dimension 0
- proj_grad: float32 [8, 128, 128], P('groups'), parts along dimension 0
There are 2 independent parts, one for each index of `groups`. A program takes and returns all parts, laid end to end along the dimension named above; an argument that names none is the same for every part. Nothing has to cross between parts.
Inputs may be any that keep to these rules, and one draw needn't show every extreme that they name: lengths[0] residues are real; those at and after index lengths[0] are padding; the two entries sum to 32.
All inputs are finite; a program needn't handle non-finite values.
Results may differ from a plain program's by a relative error of at most 0.014.
Values may be sent and summed in bfloat16 or wider, within the bound.
No kernel may reach another device: no remote copies, remote signals or barrier semaphores. Data moves between devices by JAX's collectives and lax.ppermute only.
A program may use at most 64 MiB of HBM per device.

v0:
```python
import math
import jax
import jax.numpy as jnp
from jax import lax
from jax.sharding import PartitionSpec as P

LAYERS = 4
eps = 1e-05


def with_halo(x, sides, width):
    for axis, dim in sides:
        count, length = (lax.axis_size(axis), x.shape[dim])
        up = [(i, (i + 1) % count) for i in range(count - 1)]
        down = [(j, i) for i, j in up]
        last = lax.slice_in_dim(x, length - width, length, axis=dim)
        first = lax.slice_in_dim(x, 0, width, axis=dim)
        before = lax.ppermute(last, axis, up)
        after = lax.ppermute(first, axis, down)
        x = jnp.concatenate([before, x, after], axis=dim)
    return x


def elu_slope(values):
    return jnp.where(values > 0, 1.0, jnp.exp(jnp.minimum(values, 0.0)))


def normalize(stream, gain_row):
    average = jnp.mean(stream, axis=-1, keepdims=True)
    centred = stream - average
    variance = jnp.mean(centred * centred, axis=-1, keepdims=True)
    inv_std = lax.rsqrt(variance + eps)
    normalized = centred * inv_std
    return (normalized, inv_std, normalized * gain_row)


def conv_forward(padded, weight, spacing, height, width):
    channels = padded.shape[-1]
    summed = jnp.zeros((height * width, weight.shape[-1]), jnp.float32)
    for tap_row in range(3):
        for tap_col in range(3):
            window = padded[
                tap_row * spacing : tap_row * spacing + height,
                tap_col * spacing : tap_col * spacing + width,
                :,
            ]
            summed = summed + jnp.dot(
                window.reshape(height * width, channels),
                weight[tap_row, tap_col],
                preferred_element_type=jnp.float32,
            )
    return summed.reshape(height, width, -1)


def conv_backward(padded, weight, spacing, height, width):
    channels = padded.shape[-1]
    summed = jnp.zeros((height * width, weight.shape[-2]), jnp.float32)
    for tap_row in range(3):
        for tap_col in range(3):
            start_row = (2 - tap_row) * spacing
            start_col = (2 - tap_col) * spacing
            window = padded[start_row : start_row + height, start_col : start_col + width, :]
            summed = summed + jnp.dot(
                window.reshape(height * width, channels),
                weight[tap_row, tap_col].T,
                preferred_element_type=jnp.float32,
            )
    return summed.reshape(height, width, -1)


def conv_weight_grad(padded, grad_tile, spacing, height, width):
    channels = padded.shape[-1]
    flat_grad = grad_tile.reshape(height * width, -1)
    terms = []
    for tap_row in range(3):
        row_terms = []
        for tap_col in range(3):
            window = padded[
                tap_row * spacing : tap_row * spacing + height,
                tap_col * spacing : tap_col * spacing + width,
                :,
            ]
            row_terms.append(
                lax.dot_general(
                    window.reshape(height * width, channels),
                    flat_grad,
                    (((0,), (0,)), ((), ())),
                    preferred_element_type=jnp.float32,
                )
            )
        terms.append(jnp.stack(row_terms))
    return jnp.stack(terms)


def body(seq_feat, lengths, embed_weight, norm_gain, conv_weight, proj_weight, pair_cotangent):
    tile_rows = pair_cotangent.shape[0]
    tile_cols = pair_cotangent.shape[1]
    channels = pair_cotangent.shape[2]
    residues = tile_rows * lax.axis_size("row")
    row_start = lax.axis_index("row") * tile_rows
    col_start = lax.axis_index("col") * tile_cols
    row_live = (row_start + jnp.arange(tile_rows, dtype=jnp.int32) < lengths[0]).astype(jnp.float32)
    col_live = (col_start + jnp.arange(tile_cols, dtype=jnp.int32) < lengths[0]).astype(jnp.float32)
    live_mask = row_live[:, None, None] * col_live[None, :, None]
    gathered = lax.all_gather(seq_feat, ("row", "col"), axis=0, tiled=True)
    row_part = lax.dynamic_slice_in_dim(gathered, row_start, tile_rows, 0)
    col_part = lax.dynamic_slice_in_dim(gathered, col_start, tile_cols, 0)
    row_emb = jnp.dot(row_part, embed_weight[0], preferred_element_type=jnp.float32).astype(
        jnp.bfloat16
    )
    col_emb = jnp.dot(col_part, embed_weight[1], preferred_element_type=jnp.float32).astype(
        jnp.bfloat16
    )
    stream = live_mask * (
        row_emb.astype(jnp.float32)[:, None, :] + col_emb.astype(jnp.float32)[None, :, :]
    )
    stored = []
    for layer_number in range(LAYERS):
        spacing = 2**layer_number
        normalized, inv_std, scaled = normalize(stream, norm_gain[layer_number])
        squashed = (live_mask * jax.nn.elu(scaled)).astype(jnp.bfloat16)
        padded = with_halo(squashed, (("row", 0), ("col", 1)), spacing)
        convolved = conv_forward(padded, conv_weight[layer_number], spacing, tile_rows, tile_cols)
        excited = jax.nn.elu(convolved).astype(jnp.bfloat16)
        update = jnp.dot(
            excited.reshape(-1, channels),
            proj_weight[layer_number],
            preferred_element_type=jnp.float32,
        ).reshape(tile_rows, tile_cols, channels)
        stored.append((stream, padded, convolved, excited))
        stream = stream + live_mask * update
    pair_output = stream.astype(jnp.bfloat16)
    grad_scale = 1.0 / residues
    back_grad = pair_cotangent.astype(jnp.float32)
    gain_terms = [None] * LAYERS
    conv_terms = [None] * LAYERS
    proj_terms = [None] * LAYERS
    for layer_number in reversed(range(LAYERS)):
        spacing = 2**layer_number
        old_stream, padded, convolved, excited = stored[layer_number]
        masked = (live_mask * back_grad).astype(jnp.bfloat16)
        flat_masked = masked.reshape(-1, channels)
        proj_term = (
            lax.dot_general(
                excited.reshape(-1, channels),
                flat_masked,
                (((0,), (0,)), ((), ())),
                preferred_element_type=jnp.float32,
            )
            * grad_scale
        )
        d_excited = jnp.dot(
            flat_masked, proj_weight[layer_number].T, preferred_element_type=jnp.float32
        ).reshape(tile_rows, tile_cols, channels)
        d_pre = (d_excited * elu_slope(convolved)).astype(jnp.bfloat16)
        conv_term = conv_weight_grad(padded, d_pre, spacing, tile_rows, tile_cols) * grad_scale
        d_padded = with_halo(d_pre, (("row", 0), ("col", 1)), spacing)
        d_squashed = conv_backward(
            d_padded, conv_weight[layer_number], spacing, tile_rows, tile_cols
        )
        normalized, inv_std, scaled = normalize(old_stream, norm_gain[layer_number])
        d_scaled = live_mask * d_squashed * elu_slope(scaled)
        gain_term = jnp.sum(d_scaled * normalized, axis=(0, 1)) * grad_scale
        d_norm = d_scaled * norm_gain[layer_number]
        back_grad = back_grad + inv_std * (
            d_norm
            - jnp.mean(d_norm, axis=-1, keepdims=True)
            - normalized * jnp.mean(d_norm * normalized, axis=-1, keepdims=True)
        )
        gain_terms[layer_number] = gain_term
        conv_terms[layer_number] = conv_term
        proj_terms[layer_number] = proj_term
    final_masked = live_mask * back_grad
    row_totals = jnp.sum(final_masked, axis=1)
    col_totals = jnp.sum(final_masked, axis=0)
    d_row = lax.psum_scatter(row_totals, "col", scatter_dimension=0, tiled=True).astype(
        jnp.bfloat16
    )
    spread_cols = lax.dynamic_update_slice_in_dim(
        jnp.zeros((residues, channels), jnp.float32), col_totals, col_start, 0
    )
    d_col = lax.psum_scatter(spread_cols, ("row", "col"), scatter_dimension=0, tiled=True).astype(
        jnp.bfloat16
    )
    seq_grad = (
        jnp.dot(d_row, embed_weight[0].T, preferred_element_type=jnp.float32)
        + jnp.dot(d_col, embed_weight[1].T, preferred_element_type=jnp.float32)
    ) / math.sqrt(residues)
    embed_term = (
        jnp.stack(
            [
                lax.dot_general(
                    seq_feat, d_row, (((0,), (0,)), ((), ())), preferred_element_type=jnp.float32
                ),
                lax.dot_general(
                    seq_feat, d_col, (((0,), (0,)), ((), ())), preferred_element_type=jnp.float32
                ),
            ]
        )
        * grad_scale
    )
    gain_grad = jnp.stack(gain_terms)
    conv_grad = jnp.stack(conv_terms)
    proj_grad = jnp.stack(proj_terms)
    gain_grad, conv_grad, proj_grad, embed_grad = lax.psum(
        (gain_grad, conv_grad, proj_grad, embed_term), ("row", "col")
    )
    return (pair_output, seq_grad, embed_grad, gain_grad, conv_grad, proj_grad)


def solution(mesh):
    placed = (
        P(("groups", "row", "col"), None),
        P("groups"),
        P(),
        P(),
        P(),
        P(),
        P(("groups", "row"), "col", None),
    )
    return jax.shard_map(
        body,
        mesh=mesh,
        in_specs=placed,
        out_specs=(
            P(("groups", "row"), "col", None),
            P(("groups", "row", "col"), None),
            P("groups", None, None),
            P("groups", None),
            P("groups", None, None, None, None),
            P("groups", None, None),
        ),
        check_vma=False,
    )
```

profile of v0, /device:TPU:0, one launch (start us, length us, event | category | flops | bytes accessed | tf_op | source)
XLA Modules:
  0.0 350.0 jit_solution(10148906690786767600)
XLA Ops:
  8.8 23.3 %all-gather = bf16[16,2,256]{2,1,0:T(2,128)(2,1)S(1)} all-gather(bf16[1,2,256]{2,1,0:T(2,128)(2,1)} %bitcast.781), channel_id=1, replica_groups=mesh['groups'=2,'row'=4,'col'=4] {'row','col'}, dimensions={0}, use_global_device_ids=true | all-gather | bytes 17408 | tf_op jit(solution)/shard_map/all_gather | solution.py:105
  35.9 1.3 collective-permute-start.1
  37.2 1.3 slice_bitcast_fusion
  38.5 2.9 collective-permute-done.1
  42.7 1.3 collective-permute-start.3
  44.1 1.6 collective-permute-done.3
  47.4 2.4 collective-permute-start.4
  49.7 1.3 collective-permute-start.5
  53.9 1.3 collective-permute-done.5
  55.3 2.6 collective-permute-start.6
  57.9 1.3 collective-permute-start.7
  59.3 2.4 collective-permute-done.7
  63.3 3.9 %collective-permute-start.8 = (bf16[4,8,128]{2,1,0:T(8,128)(2,1)S(1)}, bf16[4,8,128]{2,1,0:T(8,128)(2,1)S(1)}, u32[]{:S(2)}, u32[]{:S(2)}) collective-permute-start(bf16[4,8,128]{2,1,0:T(8,128)(2,1)S(1)} %get-tuple-element.67), channel_id=1, source_target_pairs={{0,4},{4,8},{8,12},{1,5},{5,9},{9,13},{2,6},{6,10},{10,14},{3,7},{... | collective-permute-start | bytes 24584 | tf_op jit(solution)/shard_map/ppermute | solution.py:18
  67.2 1.3 collective-permute-start.9
  68.6 4.1 %collective-permute-done.9 = bf16[4,8,128]{2,1,0:T(8,128)(2,1)S(1)} collective-permute-done((bf16[4,8,128]{2,1,0:T(8,128)(2,1)S(1)}, bf16[4,8,128]{2,1,0:T(8,128)(2,1)S(1)}, u32[]{:S(2)}, u32[]{:S(2)}) %collective-permute-start.9) | collective-permute-done | bytes 8224 | tf_op jit(solution)/shard_map/ppermute | solution.py:19
  72.8 2.9 collective-permute-start.10
  75.6 1.3 collective-permute-start.11
  77.2 2.5 collective-permute-done.11
  81.0 1.3 collective-permute-start.13
  82.3 4.5 %collective-permute-start.12 = (bf16[8,8,128]{2,1,0:T(8,128)(2,1)S(1)}, bf16[8,8,128]{2,1,0:T(8,128)(2,1)S(1)}, u32[]{:S(2)}, u32[]{:S(2)}) collective-permute-start(bf16[8,8,128]{2,1,0:T(8,128)(2,1)S(1)} %fusion.106), channel_id=1, source_target_pairs={{0,4},{4,8},{8,12},{1,5},{5,9},{9,13},{2,6},{6,10},{10,14},{3,7},{... | collective-permute-start | bytes 49160 | tf_op jit(solution)/shard_map/ppermute | solution.py:18
  87.0 1.3 collective-permute-done.12
  89.6 3.9 %collective-permute-start.14 = (bf16[24,8,128]{2,1,0:T(8,128)(2,1)S(1)}, bf16[24,8,128]{2,1,0:T(8,128)(2,1)S(1)}, u32[]{:S(2)}, u32[]{:S(2)}) collective-permute-start(bf16[24,8,128]{2,1,0:T(8,128)(2,1)S(1)} %pad_maximum_fusion.3), channel_id=1, source_target_pairs={{0,1},{1,2},{2,3},{4,5},{5,6},{6,7},{8,9},{9,10},{10,11},{12,13},{... | collective-permute-start | bytes 147464 | tf_op jit(solution)/shard_map/ppermute | solution.py:18
  95.1 1.3 collective-permute-start.17
  96.4 4.5 %collective-permute-start.16 = (bf16[8,8,128]{2,1,0:T(8,128)(2,1)S(1)}, bf16[8,8,128]{2,1,0:T(8,128)(2,1)S(1)}, u32[]{:S(2)}, u32[]{:S(2)}) collective-permute-start(bf16[8,8,128]{2,1,0:T(8,128)(2,1)S(1)} %fusion.50), channel_id=1, source_target_pairs={{0,4},{4,8},{8,12},{1,5},{5,9},{9,13},{2,6},{6,10},{10,14},{3,7},{... | collective-permute-start | bytes 49160 | tf_op jit(solution)/shard_map/ppermute | solution.py:18
  103.4 3.6 %collective-permute-start.19 = (bf16[24,8,128]{2,1,0:T(8,128)(2,1)S(1)}, bf16[24,8,128]{2,1,0:T(8,128)(2,1)S(1)}, u32[]{:S(2)}, u32[]{:S(2)}) collective-permute-start(bf16[24,8,128]{2,1,0:T(8,128)(2,1)S(1)} %pad_maximum_fusion.4), channel_id=1, source_target_pairs={{0,1},{1,2},{2,3},{4,5},{5,6},{6,7},{8,9},{9,10},{10,11},{12,13},{... | collective-permute-start | bytes 147464 | tf_op jit(solution)/shard_map/ppermute | solution.py:18
  107.1 1.3 collective-permute-start.18
  109.0 3.4 collective-permute-done.18
  113.7 3.9 %collective-permute-start.20 = (bf16[4,8,128]{2,1,0:T(8,128)(2,1)S(1)}, bf16[4,8,128]{2,1,0:T(8,128)(2,1)S(1)}, u32[]{:S(2)}, u32[]{:S(2)}) collective-permute-start(bf16[4,8,128]{2,1,0:T(8,128)(2,1)S(1)} %get-tuple-element.65), channel_id=1, source_target_pairs={{0,4},{4,8},{8,12},{1,5},{5,9},{9,13},{2,6},{6,10},{10,14},{3,7},{... | collective-permute-start | bytes 24584 | tf_op jit(solution)/shard_map/ppermute | solution.py:18
  117.7 1.3 collective-permute-start.21
  121.1 2.1 collective-permute-done.21
  123.2 1.3 collective-permute-start.22
  124.5 3.9 %collective-permute-start.23 = (bf16[16,4,128]{2,1,0:T(4,128)(2,1)S(1)}, bf16[16,4,128]{2,1,0:T(4,128)(2,1)S(1)}, u32[]{:S(2)}, u32[]{:S(2)}) collective-permute-start(bf16[16,4,128]{2,1,0:T(4,128)(2,1)S(1)} %get-tuple-element.42), channel_id=1, source_target_pairs={{0,1},{1,2},{2,3},{4,5},{5,6},{6,7},{8,9},{9,10},{10,11},{12,13},{... | collective-permute-start | bytes 49160 | tf_op jit(solution)/shard_map/ppermute | solution.py:18
  132.1 3.3 collective-permute-start.24
  135.4 1.3 collective-permute-start.25
  137.5 3.4 collective-permute-done.25
  140.9 1.3 collective-permute-start.26
  142.2 3.0 collective-permute-start.27
  149.5 3.3 collective-permute-start.28
  152.8 1.3 collective-permute-start.29
  154.6 1.6 pad_maximum_fusion
  156.9 1.3 collective-permute-done.29
  158.3 1.3 collective-permute-start.30
  159.6 4.6 %collective-permute-start.31 = (bf16[10,1,128]{2,1,0:T(2,128)(2,1)S(1)}, bf16[10,1,128]{2,1,0:T(2,128)(2,1)S(1)}, u32[]{:S(2)}, u32[]{:S(2)}) collective-permute-start(bf16[10,1,128]{2,1,0:T(2,128)(2,1)S(1)} %get-tuple-element.56), channel_id=1, source_target_pairs={{0,1},{1,2},{2,3},{4,5},{5,6},{6,7},{8,9},{9,10},{10,11},{12,13},{... | collective-permute-start | bytes 7688 | tf_op jit(solution)/shard_map/ppermute | solution.py:18
  166.7 9.7 %all-reduce = bf16[8,128]{1,0:T(8,128)(2,1)S(1)} all-reduce(f32[8,128]{1,0:T(8,128)S(1)} %get-tuple-element.31), channel_id=2, replica_groups=mesh['groups'=2,'row'=4,'col'=4] {'col'}, use_global_device_ids=true, to_apply=%region_17.18.clone | all-reduce | flops 1024 | bytes 6144
  176.4 59.6 %all-reduce.2 = (bf16[32,128]{1,0:T(8,128)(2,1)S(1)}, f32[4,128]{1,0:T(4,128)}) all-reduce(f32[32,128]{1,0:T(8,128)S(1)} %constant_dynamic-update-slice_fusion, f32[4,128]{1,0:T(4,128)S(1)} %pad_maximum_fusion.48), channel_id=3, replica_groups=mesh['groups'=2,'row'=4,'col'=4] {'row','col'}, use_global_device_ids=true, to_apply=%region_19.20.clone | all-reduce | flops 4608 | bytes 28672
  238.9 98.4 %all-reduce.6.cloned.1.call-done = (f32[2,256,128]{1,2,0:T(8,128)}, f32[4,3,3,128,128]{4,3,2,1,0:T(8,128)}, f32[4,128,128]{2,1,0:T(8,128)}) async-done(((f32[2,256,128]{1,2,0:T(8,128)}, f32[4,3,3,128,128]{4,3,2,1,0:T(8,128)}, f32[4,128,128]{2,1,0:T(8,128)}), (f32[2,256,128]{1,2,0:T(8,128)}, f32[4,3,3,128,128]{4,3,2,1,0:T(8,128)}, f32[4,128,128]{2,1,0:T(8,128)})) %all-reduce.6.cloned.1.call-update) | async-done | bytes 2883600 | tf_op jit(solution)/shard_map/psum | solution.py:205
  337.3 1.8 copy.14
  339.1 3.4 copy.19
  (256 shorter events, 38.6 us)
Async XLA Ops:
  7.2 44.0 %copy-start.6 = (u32[32]{0:T(128)S(1)}, u32[32]{0:T(128)}, u32[]{:S(2)}) copy-start(u32[32]{0:T(128)} %constant.72) | copy-start | bytes 388
  7.2 44.6 %copy-start.5 = (u32[32]{0:T(128)S(1)}, u32[32]{0:T(128)}, u32[]{:S(2)}) copy-start(u32[32]{0:T(128)} %constant.68) | copy-start | bytes 388
  7.2 39.7 %copy-start.1 = (bf16[4,128,128]{2,1,0:T(8,128)(2,1)S(1)}, bf16[4,128,128]{2,1,0:T(8,128)(2,1)}, u32[]{:S(2)}) copy-start(bf16[4,128,128]{2,1,0:T(8,128)(2,1)} %param.12) | copy-start | bytes 393220
  7.2 330.1 %all-reduce.6.cloned.1.call-start = ((), (), s32[]{:S(2)}) async-start(), calls=%async_computation | async-start | bytes 5767168 | tf_op jit(solution)/shard_map/psum | solution.py:205
  34.6 3.9 %collective-permute-start = (bf16[1,8,128]{2,1,0:T(8,128)(2,1)S(1)}, bf16[1,8,128]{2,1,0:T(8,128)(2,1)S(1)}, u32[]{:S(2)}, u32[]{:S(2)}) collective-permute-start(bf16[1,8,128]{2,1,0:T(8,128)(2,1)S(1)} %get-tuple-element.71), channel_id=1, source_target_pairs={{0,4},{4,8},{8,12},{1,5},{5,9},{9,13},{2,6},{6,10},{10,14},{3,7},{... | collective-permute-start | bytes 6152 | tf_op jit(solution)/shard_map/ppermute | solution.py:18
  35.9 5.5 %collective-permute-start.1 = (bf16[1,8,128]{2,1,0:T(8,128)(2,1)S(1)}, bf16[1,8,128]{2,1,0:T(8,128)(2,1)S(1)}, u32[]{:S(2)}, u32[]{:S(2)}) collective-permute-start(bf16[1,8,128]{2,1,0:T(8,128)(2,1)S(1)} %get-tuple-element.72), channel_id=1, source_target_pairs={{4,0},{8,4},{12,8},{5,1},{9,5},{13,9},{6,2},{10,6},{14,10},{7,3},{... | collective-permute-start | bytes 6152 | tf_op jit(solution)/shard_map/ppermute | solution.py:19
  41.4 2.7 collective-permute-start.2
  42.7 3.1 collective-permute-start.3
  46.7 48.2 %copy-start.3 = (bf16[8,8,128]{2,1,0:T(8,128)(2,1)S(1)}, bf16[8,8,128]{2,1,0:T(8,128)(2,1)}, u32[]{:S(2)}) copy-start(bf16[8,8,128]{2,1,0:T(8,128)(2,1)} %param.13) | copy-start | bytes 49156
  47.4 6.6 %collective-permute-start.4 = (bf16[2,8,128]{2,1,0:T(8,128)(2,1)S(1)}, bf16[2,8,128]{2,1,0:T(8,128)(2,1)S(1)}, u32[]{:S(2)}, u32[]{:S(2)}) collective-permute-start(bf16[2,8,128]{2,1,0:T(8,128)(2,1)S(1)} %get-tuple-element.69), channel_id=1, source_target_pairs={{0,4},{4,8},{8,12},{1,5},{5,9},{9,13},{2,6},{6,10},{10,14},{3,7},{... | collective-permute-start | bytes 12296 | tf_op jit(solution)/shard_map/ppermute | solution.py:18
  49.7 5.5 %collective-permute-start.5 = (bf16[2,8,128]{2,1,0:T(8,128)(2,1)S(1)}, bf16[2,8,128]{2,1,0:T(8,128)(2,1)S(1)}, u32[]{:S(2)}, u32[]{:S(2)}) collective-permute-start(bf16[2,8,128]{2,1,0:T(8,128)(2,1)S(1)} %get-tuple-element.70), channel_id=1, source_target_pairs={{4,0},{8,4},{12,8},{5,1},{9,5},{13,9},{6,2},{10,6},{14,10},{7,3},{... | collective-permute-start | bytes 12296 | tf_op jit(solution)/shard_map/ppermute | solution.py:19
  55.3 4.1 %collective-permute-start.6 = (bf16[12,2,128]{2,1,0:T(2,128)(2,1)S(1)}, bf16[12,2,128]{2,1,0:T(2,128)(2,1)S(1)}, u32[]{:S(2)}, u32[]{:S(2)}) collective-permute-start(bf16[12,2,128]{2,1,0:T(2,128)(2,1)S(1)} %get-tuple-element.51), channel_id=1, source_target_pairs={{0,1},{1,2},{2,3},{4,5},{5,6},{6,7},{8,9},{9,10},{10,11},{12,13},{... | collective-permute-start | bytes 18440 | tf_op jit(solution)/shard_map/ppermute | solution.py:18
  57.9 3.8 %collective-permute-start.7 = (bf16[12,2,128]{2,1,0:T(2,128)(2,1)S(1)}, bf16[12,2,128]{2,1,0:T(2,128)(2,1)S(1)}, u32[]{:S(2)}, u32[]{:S(2)}) collective-permute-start(bf16[12,2,128]{2,1,0:T(2,128)(2,1)S(1)} %get-tuple-element.52), channel_id=1, source_target_pairs={{1,0},{2,1},{3,2},{5,4},{6,5},{7,6},{9,8},{10,9},{11,10},{13,12},{... | collective-permute-start | bytes 18440 | tf_op jit(solution)/shard_map/ppermute | solution.py:19
  63.3 5.3 %collective-permute-start.8 = (bf16[4,8,128]{2,1,0:T(8,128)(2,1)S(1)}, bf16[4,8,128]{2,1,0:T(8,128)(2,1)S(1)}, u32[]{:S(2)}, u32[]{:S(2)}) collective-permute-start(bf16[4,8,128]{2,1,0:T(8,128)(2,1)S(1)} %get-tuple-element.67), channel_id=1, source_target_pairs={{0,4},{4,8},{8,12},{1,5},{5,9},{9,13},{2,6},{6,10},{10,14},{3,7},{... | collective-permute-start | bytes 24584 | tf_op jit(solution)/shard_map/ppermute | solution.py:18
  67.2 5.5 %collective-permute-start.9 = (bf16[4,8,128]{2,1,0:T(8,128)(2,1)S(1)}, bf16[4,8,128]{2,1,0:T(8,128)(2,1)S(1)}, u32[]{:S(2)}, u32[]{:S(2)}) collective-permute-start(bf16[4,8,128]{2,1,0:T(8,128)(2,1)S(1)} %get-tuple-element.68), channel_id=1, source_target_pairs={{4,0},{8,4},{12,8},{5,1},{9,5},{13,9},{6,2},{10,6},{14,10},{7,3},{... | collective-permute-start | bytes 24584 | tf_op jit(solution)/shard_map/ppermute | solution.py:19
  72.8 7.2 %collective-permute-start.10 = (bf16[16,4,128]{2,1,0:T(4,128)(2,1)S(1)}, bf16[16,4,128]{2,1,0:T(4,128)(2,1)S(1)}, u32[]{:S(2)}, u32[]{:S(2)}) collective-permute-start(bf16[16,4,128]{2,1,0:T(4,128)(2,1)S(1)} %get-tuple-element.43), channel_id=1, source_target_pairs={{0,1},{1,2},{2,3},{4,5},{5,6},{6,7},{8,9},{9,10},{10,11},{12,13},{... | collective-permute-start | bytes 49160 | tf_op jit(solution)/shard_map/ppermute | solution.py:18
  75.6 4.1 %collective-permute-start.11 = (bf16[16,4,128]{2,1,0:T(4,128)(2,1)S(1)}, bf16[16,4,128]{2,1,0:T(4,128)(2,1)S(1)}, u32[]{:S(2)}, u32[]{:S(2)}) collective-permute-start(bf16[16,4,128]{2,1,0:T(4,128)(2,1)S(1)} %get-tuple-element.44), channel_id=1, source_target_pairs={{1,0},{2,1},{3,2},{5,4},{6,5},{7,6},{9,8},{10,9},{11,10},{13,12},{... | collective-permute-start | bytes 49160 | tf_op jit(solution)/shard_map/ppermute | solution.py:19
  81.0 6.0 %collective-permute-start.13 = (bf16[8,8,128]{2,1,0:T(8,128)(2,1)S(1)}, bf16[8,8,128]{2,1,0:T(8,128)(2,1)S(1)}, u32[]{:S(2)}, u32[]{:S(2)}) collective-permute-start(bf16[8,8,128]{2,1,0:T(8,128)(2,1)S(1)} %fusion.106), channel_id=1, source_target_pairs={{4,0},{8,4},{12,8},{5,1},{9,5},{13,9},{6,2},{10,6},{14,10},{7,3},{... | collective-permute-start | bytes 49160 | tf_op jit(solution)/shard_map/ppermute | solution.py:19
  82.3 6.0 %collective-permute-start.12 = (bf16[8,8,128]{2,1,0:T(8,128)(2,1)S(1)}, bf16[8,8,128]{2,1,0:T(8,128)(2,1)S(1)}, u32[]{:S(2)}, u32[]{:S(2)}) collective-permute-start(bf16[8,8,128]{2,1,0:T(8,128)(2,1)S(1)} %fusion.106), channel_id=1, source_target_pairs={{0,4},{4,8},{8,12},{1,5},{5,9},{9,13},{2,6},{6,10},{10,14},{3,7},{... | collective-permute-start | bytes 49160 | tf_op jit(solution)/shard_map/ppermute | solution.py:18
  88.3 5.4 %collective-permute-start.15 = (bf16[24,8,128]{2,1,0:T(8,128)(2,1)S(1)}, bf16[24,8,128]{2,1,0:T(8,128)(2,1)S(1)}, u32[]{:S(2)}, u32[]{:S(2)}) collective-permute-start(bf16[24,8,128]{2,1,0:T(8,128)(2,1)S(1)} %pad_maximum_fusion.3), channel_id=1, source_target_pairs={{1,0},{2,1},{3,2},{5,4},{6,5},{7,6},{9,8},{10,9},{11,10},{13,12},{... | collective-permute-start | bytes 147464 | tf_op jit(solution)/shard_map/ppermute | solution.py:19
  89.6 4.7 %collective-permute-start.14 = (bf16[24,8,128]{2,1,0:T(8,128)(2,1)S(1)}, bf16[24,8,128]{2,1,0:T(8,128)(2,1)S(1)}, u32[]{:S(2)}, u32[]{:S(2)}) collective-permute-start(bf16[24,8,128]{2,1,0:T(8,128)(2,1)S(1)} %pad_maximum_fusion.3), channel_id=1, source_target_pairs={{0,1},{1,2},{2,3},{4,5},{5,6},{6,7},{8,9},{9,10},{10,11},{12,13},{... | collective-permute-start | bytes 147464 | tf_op jit(solution)/shard_map/ppermute | solution.py:18
  95.1 8.3 %collective-permute-start.17 = (bf16[8,8,128]{2,1,0:T(8,128)(2,1)S(1)}, bf16[8,8,128]{2,1,0:T(8,128)(2,1)S(1)}, u32[]{:S(2)}, u32[]{:S(2)}) collective-permute-start(bf16[8,8,128]{2,1,0:T(8,128)(2,1)S(1)} %fusion.50), channel_id=1, source_target_pairs={{4,0},{8,4},{12,8},{5,1},{9,5},{13,9},{6,2},{10,6},{14,10},{7,3},{... | collective-permute-start | bytes 49160 | tf_op jit(solution)/shard_map/ppermute | solution.py:19
  96.4 7.0 %collective-permute-start.16 = (bf16[8,8,128]{2,1,0:T(8,128)(2,1)S(1)}, bf16[8,8,128]{2,1,0:T(8,128)(2,1)S(1)}, u32[]{:S(2)}, u32[]{:S(2)}) collective-permute-start(bf16[8,8,128]{2,1,0:T(8,128)(2,1)S(1)} %fusion.50), channel_id=1, source_target_pairs={{0,4},{4,8},{8,12},{1,5},{5,9},{9,13},{2,6},{6,10},{10,14},{3,7},{... | collective-permute-start | bytes 49160 | tf_op jit(solution)/shard_map/ppermute | solution.py:18
  103.4 5.2 %collective-permute-start.19 = (bf16[24,8,128]{2,1,0:T(8,128)(2,1)S(1)}, bf16[24,8,128]{2,1,0:T(8,128)(2,1)S(1)}, u32[]{:S(2)}, u32[]{:S(2)}) collective-permute-start(bf16[24,8,128]{2,1,0:T(8,128)(2,1)S(1)} %pad_maximum_fusion.4), channel_id=1, source_target_pairs={{0,1},{1,2},{2,3},{4,5},{5,6},{6,7},{8,9},{9,10},{10,11},{12,13},{... | collective-permute-start | bytes 147464 | tf_op jit(solution)/shard_map/ppermute | solution.py:18
  107.1 5.3 %collective-permute-start.18 = (bf16[24,8,128]{2,1,0:T(8,128)(2,1)S(1)}, bf16[24,8,128]{2,1,0:T(8,128)(2,1)S(1)}, u32[]{:S(2)}, u32[]{:S(2)}) collective-permute-start(bf16[24,8,128]{2,1,0:T(8,128)(2,1)S(1)} %pad_maximum_fusion.4), channel_id=1, source_target_pairs={{1,0},{2,1},{3,2},{5,4},{6,5},{7,6},{9,8},{10,9},{11,10},{13,12},{... | collective-permute-start | bytes 147464 | tf_op jit(solution)/shard_map/ppermute | solution.py:19
  113.7 7.3 %collective-permute-start.20 = (bf16[4,8,128]{2,1,0:T(8,128)(2,1)S(1)}, bf16[4,8,128]{2,1,0:T(8,128)(2,1)S(1)}, u32[]{:S(2)}, u32[]{:S(2)}) collective-permute-start(bf16[4,8,128]{2,1,0:T(8,128)(2,1)S(1)} %get-tuple-element.65), channel_id=1, source_target_pairs={{0,4},{4,8},{8,12},{1,5},{5,9},{9,13},{2,6},{6,10},{10,14},{3,7},{... | collective-permute-start | bytes 24584 | tf_op jit(solution)/shard_map/ppermute | solution.py:18
  117.7 5.5 %collective-permute-start.21 = (bf16[4,8,128]{2,1,0:T(8,128)(2,1)S(1)}, bf16[4,8,128]{2,1,0:T(8,128)(2,1)S(1)}, u32[]{:S(2)}, u32[]{:S(2)}) collective-permute-start(bf16[4,8,128]{2,1,0:T(8,128)(2,1)S(1)} %get-tuple-element.66), channel_id=1, source_target_pairs={{4,0},{8,4},{12,8},{5,1},{9,5},{13,9},{6,2},{10,6},{14,10},{7,3},{... | collective-permute-start | bytes 24584 | tf_op jit(solution)/shard_map/ppermute | solution.py:19
  123.2 6.3 %collective-permute-start.22 = (bf16[16,4,128]{2,1,0:T(4,128)(2,1)S(1)}, bf16[16,4,128]{2,1,0:T(4,128)(2,1)S(1)}, u32[]{:S(2)}, u32[]{:S(2)}) collective-permute-start(bf16[16,4,128]{2,1,0:T(4,128)(2,1)S(1)} %get-tuple-element.41), channel_id=1, source_target_pairs={{1,0},{2,1},{3,2},{5,4},{6,5},{7,6},{9,8},{10,9},{11,10},{13,12},{... | collective-permute-start | bytes 49160 | tf_op jit(solution)/shard_map/ppermute | solution.py:19
  124.5 4.7 %collective-permute-start.23 = (bf16[16,4,128]{2,1,0:T(4,128)(2,1)S(1)}, bf16[16,4,128]{2,1,0:T(4,128)(2,1)S(1)}, u32[]{:S(2)}, u32[]{:S(2)}) collective-permute-start(bf16[16,4,128]{2,1,0:T(4,128)(2,1)S(1)} %get-tuple-element.42), channel_id=1, source_target_pairs={{0,1},{1,2},{2,3},{4,5},{5,6},{6,7},{8,9},{9,10},{10,11},{12,13},{... | collective-permute-start | bytes 49160 | tf_op jit(solution)/shard_map/ppermute | solution.py:18
  132.1 5.4 %collective-permute-start.24 = (bf16[2,8,128]{2,1,0:T(8,128)(2,1)S(1)}, bf16[2,8,128]{2,1,0:T(8,128)(2,1)S(1)}, u32[]{:S(2)}, u32[]{:S(2)}) collective-permute-start(bf16[2,8,128]{2,1,0:T(8,128)(2,1)S(1)} %get-tuple-element.63), channel_id=1, source_target_pairs={{0,4},{4,8},{8,12},{1,5},{5,9},{9,13},{2,6},{6,10},{10,14},{3,7},{... | collective-permute-start | bytes 12296 | tf_op jit(solution)/shard_map/ppermute | solution.py:18
  135.4 5.5 %collective-permute-start.25 = (bf16[2,8,128]{2,1,0:T(8,128)(2,1)S(1)}, bf16[2,8,128]{2,1,0:T(8,128)(2,1)S(1)}, u32[]{:S(2)}, u32[]{:S(2)}) collective-permute-start(bf16[2,8,128]{2,1,0:T(8,128)(2,1)S(1)} %get-tuple-element.64), channel_id=1, source_target_pairs={{4,0},{8,4},{12,8},{5,1},{9,5},{13,9},{6,2},{10,6},{14,10},{7,3},{... | collective-permute-start | bytes 12296 | tf_op jit(solution)/shard_map/ppermute | solution.py:19
  140.9 4.5 %collective-permute-start.26 = (bf16[12,2,128]{2,1,0:T(2,128)(2,1)S(1)}, bf16[12,2,128]{2,1,0:T(2,128)(2,1)S(1)}, u32[]{:S(2)}, u32[]{:S(2)}) collective-permute-start(bf16[12,2,128]{2,1,0:T(2,128)(2,1)S(1)} %get-tuple-element.47), channel_id=1, source_target_pairs={{1,0},{2,1},{3,2},{5,4},{6,5},{7,6},{9,8},{10,9},{11,10},{13,12},{... | collective-permute-start | bytes 18440 | tf_op jit(solution)/shard_map/ppermute | solution.py:19
  142.2 3.8 %collective-permute-start.27 = (bf16[12,2,128]{2,1,0:T(2,128)(2,1)S(1)}, bf16[12,2,128]{2,1,0:T(2,128)(2,1)S(1)}, u32[]{:S(2)}, u32[]{:S(2)}) collective-permute-start(bf16[12,2,128]{2,1,0:T(2,128)(2,1)S(1)} %get-tuple-element.48), channel_id=1, source_target_pairs={{0,1},{1,2},{2,3},{4,5},{5,6},{6,7},{8,9},{9,10},{10,11},{12,13},{... | collective-permute-start | bytes 18440 | tf_op jit(solution)/shard_map/ppermute | solution.py:18
  149.5 7.4 %collective-permute-start.28 = (bf16[1,8,128]{2,1,0:T(8,128)(2,1)S(1)}, bf16[1,8,128]{2,1,0:T(8,128)(2,1)S(1)}, u32[]{:S(2)}, u32[]{:S(2)}) collective-permute-start(bf16[1,8,128]{2,1,0:T(8,128)(2,1)S(1)} %get-tuple-element.61), channel_id=1, source_target_pairs={{0,4},{4,8},{8,12},{1,5},{5,9},{9,13},{2,6},{6,10},{10,14},{3,7},{... | collective-permute-start | bytes 6152 | tf_op jit(solution)/shard_map/ppermute | solution.py:18
  152.8 5.5 %collective-permute-start.29 = (bf16[1,8,128]{2,1,0:T(8,128)(2,1)S(1)}, bf16[1,8,128]{2,1,0:T(8,128)(2,1)S(1)}, u32[]{:S(2)}, u32[]{:S(2)}) collective-permute-start(bf16[1,8,128]{2,1,0:T(8,128)(2,1)S(1)} %get-tuple-element.62), channel_id=1, source_target_pairs={{4,0},{8,4},{12,8},{5,1},{9,5},{13,9},{6,2},{10,6},{14,10},{7,3},{... | collective-permute-start | bytes 6152 | tf_op jit(solution)/shard_map/ppermute | solution.py:19
  154.6 81.4 %copy-start.4 = (bf16[2,256]{1,0:T(2,128)(2,1)S(1)}, bf16[2,256]{1,0:T(2,128)(2,1)}, u32[]{:S(2)}) copy-start(bf16[2,256]{1,0:T(2,128)(2,1)} %param.7) | copy-start | bytes 3076
  158.3 6.1 %collective-permute-start.30 = (bf16[10,1,128]{2,1,0:T(2,128)(2,1)S(1)}, bf16[10,1,128]{2,1,0:T(2,128)(2,1)S(1)}, u32[]{:S(2)}, u32[]{:S(2)}) collective-permute-start(bf16[10,1,128]{2,1,0:T(2,128)(2,1)S(1)} %get-tuple-element.55), channel_id=1, source_target_pairs={{1,0},{2,1},{3,2},{5,4},{6,5},{7,6},{9,8},{10,9},{11,10},{13,12},{... | collective-permute-start | bytes 7688 | tf_op jit(solution)/shard_map/ppermute | solution.py:19
  159.6 5.4 %collective-permute-start.31 = (bf16[10,1,128]{2,1,0:T(2,128)(2,1)S(1)}, bf16[10,1,128]{2,1,0:T(2,128)(2,1)S(1)}, u32[]{:S(2)}, u32[]{:S(2)}) collective-permute-start(bf16[10,1,128]{2,1,0:T(2,128)(2,1)S(1)} %get-tuple-element.56), channel_id=1, source_target_pairs={{0,1},{1,2},{2,3},{4,5},{5,6},{6,7},{8,9},{9,10},{10,11},{12,13},{... | collective-permute-start | bytes 7688 | tf_op jit(solution)/shard_map/ppermute | solution.py:18
  165.5 72.5 %copy-start = (bf16[2,256,128]{2,1,0:T(8,128)(2,1)S(1)}, bf16[2,256,128]{2,1,0:T(8,128)(2,1)}, u32[]{:S(2)}) copy-start(bf16[2,256,128]{2,1,0:T(8,128)(2,1)} %param.9) | copy-start | bytes 393220
  339.1 3.4 copy-start.2
Sparse Core Ops, SparseCore 0:
  237.4 99.8 all-reduce.5
where the time goes:
time: 351 us; the launch traced here: 350 us
  waiting for transfers between devices  127 us (36%)
  blocking collectives  92.6 us (26%)
  starting transfers between devices  73.6 us (21%)
  matrix products  24.4 us (7%)
  between operations  16.3 us (5%)
  local copies, waits for them, and re-layouts  9.82 us (3%)
  other arithmetic  6.18 us (2%)
    psum x1, waiting for transfers between devices, body(): lax.psum((gain_grad, conv_grad, proj_grad, embed_term), ('row', 'col'))  98.4 us
    unnamed x2, blocking collectives  69.3 us
    ppermute x16, starting transfers between devices, with_halo(): before = lax.ppermute(last, axis, up)  52.9 us
    ppermute x16, waiting for transfers between devices, with_halo(): after = lax.ppermute(first, axis, down)  25 us
    all_gather x1, blocking collectives, body(): gathered = lax.all_gather(seq_feat, ('row', 'col'), axis=0, tiled=True)  23.3 us
    ppermute x16, starting transfers between devices, with_halo(): after = lax.ppermute(first, axis, down)  20.7 us
    dot_general x36, matrix products, conv_weight_grad(): lax.dot_general(window.reshape(height * width, channels), flat_grad, (((0...  7.69 us
    unnamed x20, local copies, waits for them, and re-layouts  7.07 us
  transfers between devices with their start and end apart: 33, of which 16 were waited for; matrix products, arithmetic and copies ran while one was open for 4% of the time, Pallas kernels for 0%

commit v1 on v0

--- a/solution.py
+++ b/solution.py
@@ -203,7 +203,7 @@
     conv_grad = jnp.stack(conv_terms)
     proj_grad = jnp.stack(proj_terms)
     gain_grad, conv_grad, proj_grad, embed_grad = lax.psum(
-        (gain_grad, conv_grad, proj_grad, embed_term), ("row", "col")
+        lax.psum((gain_grad, conv_grad, proj_grad, embed_term), "col"), "row"
     )
     return (pair_output, seq_grad, embed_grad, gain_grad, conv_grad, proj_grad)
 

time: 351 us -> 428 us (1.22)
  waiting for transfers between devices: 127 us -> 192 us
  blocking collectives: 92.6 us -> 104 us
    psum x1 -> x2, waiting for transfers between devices: 98.4 us -> 164 us  [the longest x1 102 us: body(): lax.psum(lax.psum((gain_grad, conv_grad, proj_grad, embed_term), 'col'),...]
    psum x0 -> x1, blocking collectives: none -> 12.4 us  [body(): lax.psum(lax.psum((gain_grad, conv_grad, proj_grad, embed_term), 'col'),...]
  transfers between devices with their start and end apart: 33 -> 34, of which waited for: 16 -> 17; matrix products, arithmetic and copies ran while one was open for 4% -> 4% of each run, Pallas kernels for 0% -> 0%
where the time goes in v1:
time: 428 us; the launch traced here: 427 us
  waiting for transfers between devices  192 us (45%)
  blocking collectives  104 us (24%)
  starting transfers between devices  73.7 us (17%)
  matrix products  24.4 us (6%)
  between operations  16.3 us (4%)
  local copies, waits for them, and re-layouts  9.83 us (2%)
  other arithmetic  6.18 us (1%)
    psum x1, waiting for transfers between devices, body(): lax.psum(lax.psum((gain_grad, conv_grad, proj_grad, embed_term), 'col'),...  102 us
    unnamed x2, blocking collectives  68.3 us
    psum x1, waiting for transfers between devices, body(): lax.psum((gain_grad, conv_grad, proj_grad, embed_term), 'col')  61.9 us
    ppermute x16, starting transfers between devices, with_halo(): before = lax.ppermute(last, axis, up)  52.9 us
    ppermute x16, waiting for transfers between devices, with_halo(): after = lax.ppermute(first, axis, down)  25 us
    all_gather x1, blocking collectives, body(): gathered = lax.all_gather(seq_feat, ('row', 'col'), axis=0, tiled=True)  23.3 us
    ppermute x16, starting transfers between devices, with_halo(): after = lax.ppermute(first, axis, down)  20.7 us
    psum x1, blocking collectives, body(): lax.psum(lax.psum((gain_grad, conv_grad, proj_grad, embed_term), 'col'),...  12.4 us
  transfers between devices with their start and end apart: 34, of which 17 were waited for; matrix products, arithmetic and copies ran while one was open for 4% of the time, Pallas kernels for 0%

profile of v1, /device:TPU:0, one launch (start us, length us, event | category | flops | bytes accessed | tf_op | source)
XLA Modules:
  0.0 426.8 jit_solution(16562756680698050558)
XLA Ops:
  8.8 23.3 %all-gather = bf16[16,2,256]{2,1,0:T(2,128)(2,1)S(1)} all-gather(bf16[1,2,256]{2,1,0:T(2,128)(2,1)} %bitcast.781), channel_id=1, replica_groups=mesh['groups'=2,'row'=4,'col'=4] {'row','col'}, dimensions={0}, use_global_device_ids=true | all-gather | bytes 17408 | tf_op jit(solution)/shard_map/all_gather | solution.py:105
  35.9 1.3 collective-permute-start.1
  37.2 1.3 slice_bitcast_fusion
  38.5 2.9 collective-permute-done.1
  42.7 1.3 collective-permute-start.3
  44.1 1.6 collective-permute-done.3
  47.4 2.4 collective-permute-start.4
  49.7 1.3 collective-permute-start.5
  53.9 1.3 collective-permute-done.5
  55.3 2.6 collective-permute-start.6
  57.9 1.3 collective-permute-start.7
  59.3 2.4 collective-permute-done.7
  63.3 3.9 collective-permute-start.8
  67.2 1.3 collective-permute-start.9
  68.6 4.1 collective-permute-done.9
  72.8 2.9 collective-permute-start.10
  75.6 1.3 collective-permute-start.11
  77.2 2.5 collective-permute-done.11
  81.0 1.3 collective-permute-start.13
  82.3 4.5 %collective-permute-start.12 = (bf16[8,8,128]{2,1,0:T(8,128)(2,1)S(1)}, bf16[8,8,128]{2,1,0:T(8,128)(2,1)S(1)}, u32[]{:S(2)}, u32[]{:S(2)}) collective-permute-start(bf16[8,8,128]{2,1,0:T(8,128)(2,1)S(1)} %fusion.106), channel_id=1, source_target_pairs={{0,4},{4,8},{8,12},{1,5},{5,9},{9,13},{2,6},{6,10},{10,14},{3,7},{... | collective-permute-start | bytes 49160 | tf_op jit(solution)/shard_map/ppermute | solution.py:18
  87.0 1.3 collective-permute-done.12
  89.6 3.9 collective-permute-start.14
  95.1 1.3 collective-permute-start.17
  96.4 4.5 %collective-permute-start.16 = (bf16[8,8,128]{2,1,0:T(8,128)(2,1)S(1)}, bf16[8,8,128]{2,1,0:T(8,128)(2,1)S(1)}, u32[]{:S(2)}, u32[]{:S(2)}) collective-permute-start(bf16[8,8,128]{2,1,0:T(8,128)(2,1)S(1)} %fusion.50), channel_id=1, source_target_pairs={{0,4},{4,8},{8,12},{1,5},{5,9},{9,13},{2,6},{6,10},{10,14},{3,7},{... | collective-permute-start | bytes 49160 | tf_op jit(solution)/shard_map/ppermute | solution.py:18
  103.4 3.6 collective-permute-start.19
  107.1 1.3 collective-permute-start.18
  109.0 3.4 collective-permute-done.18
  113.7 3.9 collective-permute-start.20
  117.7 1.3 collective-permute-start.21
  121.1 2.1 collective-permute-done.21
  123.2 1.3 collective-permute-start.22
  124.5 3.9 collective-permute-start.23
  132.1 3.3 collective-permute-start.24
  135.4 1.3 collective-permute-start.25
  137.5 3.4 collective-permute-done.25
  140.9 1.3 collective-permute-start.26
  142.2 3.0 collective-permute-start.27
  149.5 3.3 collective-permute-start.28
  154.6 1.6 pad_maximum_fusion
  156.9 1.3 collective-permute-done.29
  159.6 4.6 %collective-permute-start.31 = (bf16[10,1,128]{2,1,0:T(2,128)(2,1)S(1)}, bf16[10,1,128]{2,1,0:T(2,128)(2,1)S(1)}, u32[]{:S(2)}, u32[]{:S(2)}) collective-permute-start(bf16[10,1,128]{2,1,0:T(2,128)(2,1)S(1)} %get-tuple-element.59), channel_id=1, source_target_pairs={{0,1},{1,2},{2,3},{4,5},{5,6},{6,7},{8,9},{9,10},{10,11},{12,13},{... | collective-permute-start | bytes 7688 | tf_op jit(solution)/shard_map/ppermute | solution.py:18
  166.7 62.4 %all-reduce.1 = bf16[32,128]{1,0:T(8,128)(2,1)S(1)} all-reduce(f32[32,128]{1,0:T(8,128)S(1)} %constant_dynamic-update-slice_fusion), channel_id=3, replica_groups=mesh['groups'=2,'row'=4,'col'=4] {'row','col'}, use_global_device_ids=true, to_apply=%region_19.20.clone | all-reduce | flops 4096 | bytes 24576
  229.2 5.8 %all-reduce.2 = (bf16[8,128]{1,0:T(8,128)(2,1)S(1)}, f32[4,128]{1,0:T(4,128)S(1)}) all-reduce(f32[8,128]{1,0:T(8,128)S(1)} %get-tuple-element.31, f32[4,128]{1,0:T(4,128)S(1)} %pad_maximum_fusion.48), channel_id=2, replica_groups=mesh['groups'=2,'row'=4,'col'=4] {'col'}, use_global_device_ids=true, to_apply=%region_17.18.clone | all-reduce | flops 1536 | bytes 10240
  236.3 61.9 %all-reduce.8.cloned.1.call-done = (f32[2,256,128]{1,2,0:T(8,128)}, f32[4,3,3,128,128]{4,3,2,1,0:T(8,128)}, f32[4,128,128]{2,1,0:T(8,128)}) async-done(((f32[2,256,128]{1,2,0:T(8,128)}, f32[4,3,3,128,128]{4,3,2,1,0:T(8,128)}, f32[4,128,128]{2,1,0:T(8,128)}), (f32[2,256,128]{1,2,0:T(8,128)}, f32[4,3,3,128,128]{4,3,2,1,0:T(8,128)}, f32[4,128,128]{2,1,0:T(8,128)})) %all-reduce.8.cloned.1.call-update) | async-done | bytes 2883600 | tf_op jit(solution)/shard_map/psum | solution.py:206
  299.0 12.4 %psum.59 = f32[4,128]{1,0:T(4,128)} all-reduce(f32[4,128]{1,0:T(4,128)S(1)} %get-tuple-element.33), channel_id=1, replica_groups=mesh['groups'=2,'row'=4,'col'=4] {'row'}, use_global_device_ids=true, to_apply=%region_27.28 | all-reduce | flops 512 | bytes 4096 | tf_op jit(solution)/shard_map/psum | solution.py:205
  312.2 101.9 %all-reduce.10.cloned.1.call-done = (f32[2,256,128]{1,2,0:T(8,128)}, f32[4,3,3,128,128]{4,3,2,1,0:T(8,128)}, f32[4,128,128]{2,1,0:T(8,128)}) async-done(((f32[2,256,128]{1,2,0:T(8,128)}, f32[4,3,3,128,128]{4,3,2,1,0:T(8,128)}, f32[4,128,128]{2,1,0:T(8,128)}), (f32[2,256,128]{1,2,0:T(8,128)}, f32[4,3,3,128,128]{4,3,2,1,0:T(8,128)}, f32[4,128,128]{2,1,0:T(8,128)})) %all-reduce.10.cloned.1.call-update) | async-done | bytes 2883600 | tf_op jit(solution)/shard_map/psum | solution.py:205
  414.1 1.8 copy.14
  415.9 3.4 copy.22
  (260 shorter events, 41.2 us)
Async XLA Ops:
  7.2 44.0 %copy-start.6 = (u32[32]{0:T(128)S(1)}, u32[32]{0:T(128)}, u32[]{:S(2)}) copy-start(u32[32]{0:T(128)} %constant.72) | copy-start | bytes 388
  7.2 44.6 %copy-start.5 = (u32[32]{0:T(128)S(1)}, u32[32]{0:T(128)}, u32[]{:S(2)}) copy-start(u32[32]{0:T(128)} %constant.68) | copy-start | bytes 388
  7.2 39.7 %copy-start.1 = (bf16[4,128,128]{2,1,0:T(8,128)(2,1)S(1)}, bf16[4,128,128]{2,1,0:T(8,128)(2,1)}, u32[]{:S(2)}) copy-start(bf16[4,128,128]{2,1,0:T(8,128)(2,1)} %param.12) | copy-start | bytes 393220
  7.2 291.0 %all-reduce.8.cloned.1.call-start = ((), (), s32[]{:S(2)}) async-start(), calls=%async_computation | async-start | bytes 5767168 | tf_op jit(solution)/shard_map/psum | solution.py:206
  34.6 3.9 collective-permute-start
  35.9 5.5 %collective-permute-start.1 = (bf16[1,8,128]{2,1,0:T(8,128)(2,1)S(1)}, bf16[1,8,128]{2,1,0:T(8,128)(2,1)S(1)}, u32[]{:S(2)}, u32[]{:S(2)}) collective-permute-start(bf16[1,8,128]{2,1,0:T(8,128)(2,1)S(1)} %get-tuple-element.75), channel_id=1, source_target_pairs={{4,0},{8,4},{12,8},{5,1},{9,5},{13,9},{6,2},{10,6},{14,10},{7,3},{... | collective-permute-start | bytes 6152 | tf_op jit(solution)/shard_map/ppermute | solution.py:19
  41.4 2.7 collective-permute-start.2
  42.7 3.1 collective-permute-start.3
  46.7 48.2 %copy-start.3 = (bf16[8,8,128]{2,1,0:T(8,128)(2,1)S(1)}, bf16[8,8,128]{2,1,0:T(8,128)(2,1)}, u32[]{:S(2)}) copy-start(bf16[8,8,128]{2,1,0:T(8,128)(2,1)} %param.13) | copy-start | bytes 49156
  47.4 6.6 %collective-permute-start.4 = (bf16[2,8,128]{2,1,0:T(8,128)(2,1)S(1)}, bf16[2,8,128]{2,1,0:T(8,128)(2,1)S(1)}, u32[]{:S(2)}, u32[]{:S(2)}) collective-permute-start(bf16[2,8,128]{2,1,0:T(8,128)(2,1)S(1)} %get-tuple-element.72), channel_id=1, source_target_pairs={{0,4},{4,8},{8,12},{1,5},{5,9},{9,13},{2,6},{6,10},{10,14},{3,7},{... | collective-permute-start | bytes 12296 | tf_op jit(solution)/shard_map/ppermute | solution.py:18
  49.7 5.5 %collective-permute-start.5 = (bf16[2,8,128]{2,1,0:T(8,128)(2,1)S(1)}, bf16[2,8,128]{2,1,0:T(8,128)(2,1)S(1)}, u32[]{:S(2)}, u32[]{:S(2)}) collective-permute-start(bf16[2,8,128]{2,1,0:T(8,128)(2,1)S(1)} %get-tuple-element.73), channel_id=1, source_target_pairs={{4,0},{8,4},{12,8},{5,1},{9,5},{13,9},{6,2},{10,6},{14,10},{7,3},{... | collective-permute-start | bytes 12296 | tf_op jit(solution)/shard_map/ppermute | solution.py:19
  55.3 4.1 collective-permute-start.6
  57.9 3.8 collective-permute-start.7
  63.3 5.3 %collective-permute-start.8 = (bf16[4,8,128]{2,1,0:T(8,128)(2,1)S(1)}, bf16[4,8,128]{2,1,0:T(8,128)(2,1)S(1)}, u32[]{:S(2)}, u32[]{:S(2)}) collective-permute-start(bf16[4,8,128]{2,1,0:T(8,128)(2,1)S(1)} %get-tuple-element.70), channel_id=1, source_target_pairs={{0,4},{4,8},{8,12},{1,5},{5,9},{9,13},{2,6},{6,10},{10,14},{3,7},{... | collective-permute-start | bytes 24584 | tf_op jit(solution)/shard_map/ppermute | solution.py:18
  67.2 5.5 %collective-permute-start.9 = (bf16[4,8,128]{2,1,0:T(8,128)(2,1)S(1)}, bf16[4,8,128]{2,1,0:T(8,128)(2,1)S(1)}, u32[]{:S(2)}, u32[]{:S(2)}) collective-permute-start(bf16[4,8,128]{2,1,0:T(8,128)(2,1)S(1)} %get-tuple-element.71), channel_id=1, source_target_pairs={{4,0},{8,4},{12,8},{5,1},{9,5},{13,9},{6,2},{10,6},{14,10},{7,3},{... | collective-permute-start | bytes 24584 | tf_op jit(solution)/shard_map/ppermute | solution.py:19
  72.8 7.2 %collective-permute-start.10 = (bf16[16,4,128]{2,1,0:T(4,128)(2,1)S(1)}, bf16[16,4,128]{2,1,0:T(4,128)(2,1)S(1)}, u32[]{:S(2)}, u32[]{:S(2)}) collective-permute-start(bf16[16,4,128]{2,1,0:T(4,128)(2,1)S(1)} %get-tuple-element.46), channel_id=1, source_target_pairs={{0,1},{1,2},{2,3},{4,5},{5,6},{6,7},{8,9},{9,10},{10,11},{12,13},{... | collective-permute-start | bytes 49160 | tf_op jit(solution)/shard_map/ppermute | solution.py:18
  75.6 4.1 collective-permute-start.11
  81.0 6.0 %collective-permute-start.13 = (bf16[8,8,128]{2,1,0:T(8,128)(2,1)S(1)}, bf16[8,8,128]{2,1,0:T(8,128)(2,1)S(1)}, u32[]{:S(2)}, u32[]{:S(2)}) collective-permute-start(bf16[8,8,128]{2,1,0:T(8,128)(2,1)S(1)} %fusion.106), channel_id=1, source_target_pairs={{4,0},{8,4},{12,8},{5,1},{9,5},{13,9},{6,2},{10,6},{14,10},{7,3},{... | collective-permute-start | bytes 49160 | tf_op jit(solution)/shard_map/ppermute | solution.py:19
  82.3 6.0 %collective-permute-start.12 = (bf16[8,8,128]{2,1,0:T(8,128)(2,1)S(1)}, bf16[8,8,128]{2,1,0:T(8,128)(2,1)S(1)}, u32[]{:S(2)}, u32[]{:S(2)}) collective-permute-start(bf16[8,8,128]{2,1,0:T(8,128)(2,1)S(1)} %fusion.106), channel_id=1, source_target_pairs={{0,4},{4,8},{8,12},{1,5},{5,9},{9,13},{2,6},{6,10},{10,14},{3,7},{... | collective-permute-start | bytes 49160 | tf_op jit(solution)/shard_map/ppermute | solution.py:18
  88.3 5.4 %collective-permute-start.15 = (bf16[24,8,128]{2,1,0:T(8,128)(2,1)S(1)}, bf16[24,8,128]{2,1,0:T(8,128)(2,1)S(1)}, u32[]{:S(2)}, u32[]{:S(2)}) collective-permute-start(bf16[24,8,128]{2,1,0:T(8,128)(2,1)S(1)} %pad_maximum_fusion.3), channel_id=1, source_target_pairs={{1,0},{2,1},{3,2},{5,4},{6,5},{7,6},{9,8},{10,9},{11,10},{13,12},{... | collective-permute-start | bytes 147464 | tf_op jit(solution)/shard_map/ppermute | solution.py:19
  89.6 4.7 %collective-permute-start.14 = (bf16[24,8,128]{2,1,0:T(8,128)(2,1)S(1)}, bf16[24,8,128]{2,1,0:T(8,128)(2,1)S(1)}, u32[]{:S(2)}, u32[]{:S(2)}) collective-permute-start(bf16[24,8,128]{2,1,0:T(8,128)(2,1)S(1)} %pad_maximum_fusion.3), channel_id=1, source_target_pairs={{0,1},{1,2},{2,3},{4,5},{5,6},{6,7},{8,9},{9,10},{10,11},{12,13},{... | collective-permute-start | bytes 147464 | tf_op jit(solution)/shard_map/ppermute | solution.py:18
  95.1 8.3 %collective-permute-start.17 = (bf16[8,8,128]{2,1,0:T(8,128)(2,1)S(1)}, bf16[8,8,128]{2,1,0:T(8,128)(2,1)S(1)}, u32[]{:S(2)}, u32[]{:S(2)}) collective-permute-start(bf16[8,8,128]{2,1,0:T(8,128)(2,1)S(1)} %fusion.50), channel_id=1, source_target_pairs={{4,0},{8,4},{12,8},{5,1},{9,5},{13,9},{6,2},{10,6},{14,10},{7,3},{... | collective-permute-start | bytes 49160 | tf_op jit(solution)/shard_map/ppermute | solution.py:19
  96.4 7.0 %collective-permute-start.16 = (bf16[8,8,128]{2,1,0:T(8,128)(2,1)S(1)}, bf16[8,8,128]{2,1,0:T(8,128)(2,1)S(1)}, u32[]{:S(2)}, u32[]{:S(2)}) collective-permute-start(bf16[8,8,128]{2,1,0:T(8,128)(2,1)S(1)} %fusion.50), channel_id=1, source_target_pairs={{0,4},{4,8},{8,12},{1,5},{5,9},{9,13},{2,6},{6,10},{10,14},{3,7},{... | collective-permute-start | bytes 49160 | tf_op jit(solution)/shard_map/ppermute | solution.py:18
  103.4 5.2 %collective-permute-start.19 = (bf16[24,8,128]{2,1,0:T(8,128)(2,1)S(1)}, bf16[24,8,128]{2,1,0:T(8,128)(2,1)S(1)}, u32[]{:S(2)}, u32[]{:S(2)}) collective-permute-start(bf16[24,8,128]{2,1,0:T(8,128)(2,1)S(1)} %pad_maximum_fusion.4), channel_id=1, source_target_pairs={{0,1},{1,2},{2,3},{4,5},{5,6},{6,7},{8,9},{9,10},{10,11},{12,13},{... | collective-permute-start | bytes 147464 | tf_op jit(solution)/shard_map/ppermute | solution.py:18
  107.1 5.3 %collective-permute-start.18 = (bf16[24,8,128]{2,1,0:T(8,128)(2,1)S(1)}, bf16[24,8,128]{2,1,0:T(8,128)(2,1)S(1)}, u32[]{:S(2)}, u32[]{:S(2)}) collective-permute-start(bf16[24,8,128]{2,1,0:T(8,128)(2,1)S(1)} %pad_maximum_fusion.4), channel_id=1, source_target_pairs={{1,0},{2,1},{3,2},{5,4},{6,5},{7,6},{9,8},{10,9},{11,10},{13,12},{... | collective-permute-start | bytes 147464 | tf_op jit(solution)/shard_map/ppermute | solution.py:19
  113.7 7.3 %collective-permute-start.20 = (bf16[4,8,128]{2,1,0:T(8,128)(2,1)S(1)}, bf16[4,8,128]{2,1,0:T(8,128)(2,1)S(1)}, u32[]{:S(2)}, u32[]{:S(2)}) collective-permute-start(bf16[4,8,128]{2,1,0:T(8,128)(2,1)S(1)} %get-tuple-element.68), channel_id=1, source_target_pairs={{0,4},{4,8},{8,12},{1,5},{5,9},{9,13},{2,6},{6,10},{10,14},{3,7},{... | collective-permute-start | bytes 24584 | tf_op jit(solution)/shard_map/ppermute | solution.py:18
  117.7 5.5 %collective-permute-start.21 = (bf16[4,8,128]{2,1,0:T(8,128)(2,1)S(1)}, bf16[4,8,128]{2,1,0:T(8,128)(2,1)S(1)}, u32[]{:S(2)}, u32[]{:S(2)}) collective-permute-start(bf16[4,8,128]{2,1,0:T(8,128)(2,1)S(1)} %get-tuple-element.69), channel_id=1, source_target_pairs={{4,0},{8,4},{12,8},{5,1},{9,5},{13,9},{6,2},{10,6},{14,10},{7,3},{... | collective-permute-start | bytes 24584 | tf_op jit(solution)/shard_map/ppermute | solution.py:19
  123.2 6.3 %collective-permute-start.22 = (bf16[16,4,128]{2,1,0:T(4,128)(2,1)S(1)}, bf16[16,4,128]{2,1,0:T(4,128)(2,1)S(1)}, u32[]{:S(2)}, u32[]{:S(2)}) collective-permute-start(bf16[16,4,128]{2,1,0:T(4,128)(2,1)S(1)} %get-tuple-element.44), channel_id=1, source_target_pairs={{1,0},{2,1},{3,2},{5,4},{6,5},{7,6},{9,8},{10,9},{11,10},{13,12},{... | collective-permute-start | bytes 49160 | tf_op jit(solution)/shard_map/ppermute | solution.py:19
  124.5 4.7 %collective-permute-start.23 = (bf16[16,4,128]{2,1,0:T(4,128)(2,1)S(1)}, bf16[16,4,128]{2,1,0:T(4,128)(2,1)S(1)}, u32[]{:S(2)}, u32[]{:S(2)}) collective-permute-start(bf16[16,4,128]{2,1,0:T(4,128)(2,1)S(1)} %get-tuple-element.45), channel_id=1, source_target_pairs={{0,1},{1,2},{2,3},{4,5},{5,6},{6,7},{8,9},{9,10},{10,11},{12,13},{... | collective-permute-start | bytes 49160 | tf_op jit(solution)/shard_map/ppermute | solution.py:18
  132.1 5.4 %collective-permute-start.24 = (bf16[2,8,128]{2,1,0:T(8,128)(2,1)S(1)}, bf16[2,8,128]{2,1,0:T(8,128)(2,1)S(1)}, u32[]{:S(2)}, u32[]{:S(2)}) collective-permute-start(bf16[2,8,128]{2,1,0:T(8,128)(2,1)S(1)} %get-tuple-element.66), channel_id=1, source_target_pairs={{0,4},{4,8},{8,12},{1,5},{5,9},{9,13},{2,6},{6,10},{10,14},{3,7},{... | collective-permute-start | bytes 12296 | tf_op jit(solution)/shard_map/ppermute | solution.py:18
  135.4 5.5 %collective-permute-start.25 = (bf16[2,8,128]{2,1,0:T(8,128)(2,1)S(1)}, bf16[2,8,128]{2,1,0:T(8,128)(2,1)S(1)}, u32[]{:S(2)}, u32[]{:S(2)}) collective-permute-start(bf16[2,8,128]{2,1,0:T(8,128)(2,1)S(1)} %get-tuple-element.67), channel_id=1, source_target_pairs={{4,0},{8,4},{12,8},{5,1},{9,5},{13,9},{6,2},{10,6},{14,10},{7,3},{... | collective-permute-start | bytes 12296 | tf_op jit(solution)/shard_map/ppermute | solution.py:19
  140.9 4.5 %collective-permute-start.26 = (bf16[12,2,128]{2,1,0:T(2,128)(2,1)S(1)}, bf16[12,2,128]{2,1,0:T(2,128)(2,1)S(1)}, u32[]{:S(2)}, u32[]{:S(2)}) collective-permute-start(bf16[12,2,128]{2,1,0:T(2,128)(2,1)S(1)} %get-tuple-element.50), channel_id=1, source_target_pairs={{1,0},{2,1},{3,2},{5,4},{6,5},{7,6},{9,8},{10,9},{11,10},{13,12},{... | collective-permute-start | bytes 18440 | tf_op jit(solution)/shard_map/ppermute | solution.py:19
  142.2 3.8 collective-permute-start.27
  149.5 7.4 %collective-permute-start.28 = (bf16[1,8,128]{2,1,0:T(8,128)(2,1)S(1)}, bf16[1,8,128]{2,1,0:T(8,128)(2,1)S(1)}, u32[]{:S(2)}, u32[]{:S(2)}) collective-permute-start(bf16[1,8,128]{2,1,0:T(8,128)(2,1)S(1)} %get-tuple-element.64), channel_id=1, source_target_pairs={{0,4},{4,8},{8,12},{1,5},{5,9},{9,13},{2,6},{6,10},{10,14},{3,7},{... | collective-permute-start | bytes 6152 | tf_op jit(solution)/shard_map/ppermute | solution.py:18
  152.8 5.5 %collective-permute-start.29 = (bf16[1,8,128]{2,1,0:T(8,128)(2,1)S(1)}, bf16[1,8,128]{2,1,0:T(8,128)(2,1)S(1)}, u32[]{:S(2)}, u32[]{:S(2)}) collective-permute-start(bf16[1,8,128]{2,1,0:T(8,128)(2,1)S(1)} %get-tuple-element.65), channel_id=1, source_target_pairs={{4,0},{8,4},{12,8},{5,1},{9,5},{13,9},{6,2},{10,6},{14,10},{7,3},{... | collective-permute-start | bytes 6152 | tf_op jit(solution)/shard_map/ppermute | solution.py:19
  154.6 80.4 %copy-start.4 = (bf16[2,256]{1,0:T(2,128)(2,1)S(1)}, bf16[2,256]{1,0:T(2,128)(2,1)}, u32[]{:S(2)}) copy-start(bf16[2,256]{1,0:T(2,128)(2,1)} %param.7) | copy-start | bytes 3076
  158.3 6.1 %collective-permute-start.30 = (bf16[10,1,128]{2,1,0:T(2,128)(2,1)S(1)}, bf16[10,1,128]{2,1,0:T(2,128)(2,1)S(1)}, u32[]{:S(2)}, u32[]{:S(2)}) collective-permute-start(bf16[10,1,128]{2,1,0:T(2,128)(2,1)S(1)} %get-tuple-element.58), channel_id=1, source_target_pairs={{1,0},{2,1},{3,2},{5,4},{6,5},{7,6},{9,8},{10,9},{11,10},{13,12},{... | collective-permute-start | bytes 7688 | tf_op jit(solution)/shard_map/ppermute | solution.py:19
  159.6 5.4 %collective-permute-start.31 = (bf16[10,1,128]{2,1,0:T(2,128)(2,1)S(1)}, bf16[10,1,128]{2,1,0:T(2,128)(2,1)S(1)}, u32[]{:S(2)}, u32[]{:S(2)}) collective-permute-start(bf16[10,1,128]{2,1,0:T(2,128)(2,1)S(1)} %get-tuple-element.59), channel_id=1, source_target_pairs={{0,1},{1,2},{2,3},{4,5},{5,6},{6,7},{8,9},{9,10},{10,11},{12,13},{... | collective-permute-start | bytes 7688 | tf_op jit(solution)/shard_map/ppermute | solution.py:18
  236.2 75.2 %copy-start = (bf16[2,256,128]{2,1,0:T(8,128)(2,1)S(1)}, bf16[2,256,128]{2,1,0:T(8,128)(2,1)}, u32[]{:S(2)}) copy-start(bf16[2,256,128]{2,1,0:T(8,128)(2,1)} %param.9) | copy-start | bytes 393220
  236.2 177.9 %all-reduce.10.cloned.1.call-start = ((), (), s32[]{:S(2)}) async-start(), calls=%async_computation.1 | async-start | bytes 5767168 | tf_op jit(solution)/shard_map/psum | solution.py:205
  415.9 3.4 copy-start.2
Sparse Core Ops, SparseCore 0:
  236.3 61.8 all-reduce.7
  300.8 113.3 all-reduce.9
